TPU v7x, 32 devices: a whole 2x2x4 slice. The times are simulated.
32 devices in a mesh: leaf: 4 (over z), front: 8 (over y, x, core).
Axes of the slice: x: 2, y: 2, z: 4, core: 2. Of those that a mesh axis runs over, the one named last changes fastest.
Arguments:
- rhs_leaf: float32 [4, 2048, 64], P('leaf', 'front'), may hold values from -2.4 to 2.4
- diag_inv: bfloat16 [4, 8, 256, 256], P('leaf', 'front'), as said below
- sub_block: bfloat16 [4, 8, 256, 256], P('leaf', 'front'), as said below
- coupling: bfloat16 [4, 256, 2048], P('leaf', None, 'front'), may hold values from -0.25 to 0.25
- update_rows: int32 [4, 256], P('leaf'), may hold values from 0 to 1023, as said below
- rhs_sep: float32 [1024, 64], P('leaf'), may hold values from -6 to 6
- sep_inv: bfloat16 [1024, 1024], P('front', 'leaf'), as said below
Outputs:
- leaf_solution: float32 [4, 2048, 64], P('leaf', 'front')
- separator_solution: float32 [1024, 64], P('leaf')
Inputs may be any that keep to these rules, and one draw needn't show every extreme that they name: `update_rows`: within a group the 256 indices are distinct and increasing, and include the first and the last separator row. `diag_inv`: each 256 x 256 block is lower triangular. `sub_block`: each 256 x 256 block is lower triangular. `sep_inv`: lower triangular.
All inputs are finite; a program needn't handle non-finite values.
Results may differ from a plain program's by a relative error of at most 0.0003.
Values may be sent and summed in bfloat16 or wider, within the bound.
A program may use at most 64 MiB of HBM per device.

v0:
```python
import jax
import jax.numpy as jnp
from jax import lax
from jax.sharding import PartitionSpec as P

S = 1024


PRECISE = lax.Precision.HIGHEST


def carried_in(value, axis, join, neutral, backward):
    count, mine = (lax.axis_size(axis), lax.axis_index(axis))
    pieces = jax.tree.map(lambda part: lax.all_gather(part, axis), value)
    if backward:
        pieces = jax.tree.map(lambda part: part[::-1], pieces)
        mine = count - 1 - mine
    total = jax.tree.map(
        lambda part, zero: jnp.full_like(part, 0) + jnp.asarray(zero, part.dtype), value, neutral
    )

    def step(position, total):
        longer = join(total, jax.tree.map(lambda part: part[position], pieces))
        return jax.tree.map(lambda new, old: jnp.where(position < mine, new, old), longer, total)

    return lax.fori_loop(0, count - 1, step, total)


def shifted_2(value, axis, steps):
    count = lax.axis_size(axis)
    initial, last = (max(0, -steps), min(count, count - steps))
    return lax.ppermute(value, axis, [(source, source + steps) for source in range(initial, last)])


def product(left, right):
    return jnp.matmul(left, right, precision=PRECISE)


def narrow_product(left, right):
    return jnp.dot(left, right, preferred_element_type=jnp.float32)


def compose(earlier, later):
    return (product(later[0], earlier[0]), product(later[0], earlier[1]) + later[1])


def apply_maps(state, inputs):
    step_map, offset = inputs
    value = product(step_map, state) + offset
    return (value, value)


def forward_maps(carry, inputs):
    inverse, couple, right = inputs
    step_map = -narrow_product(inverse, couple)
    offset = product(inverse.astype(jnp.float32), right)
    mapped, shifted = carry
    return ((product(step_map, mapped), product(step_map, shifted) + offset), (step_map, offset))


def backward_maps(carry, inputs):
    inverse, couple, right = inputs
    step_map = -narrow_product(couple, inverse).T
    offset = product(inverse.astype(jnp.float32).T, right)
    mapped, shifted = carry
    return ((product(step_map, mapped), product(step_map, shifted) + offset), (step_map, offset))


def shards(rhs_leaf, diag_inv, sub_block, coupling, update_rows, rhs_sep, sep_inv):
    count = diag_inv.shape[1]
    width = diag_inv.shape[2]
    columns = rhs_leaf.shape[2]
    identity_w = jnp.eye(width, dtype=jnp.float32)
    zero_state = jnp.zeros((width, columns), jnp.float32)
    blocks = rhs_leaf[0].reshape(count, width, columns)
    (whole_map, whole_shift), (maps_fwd, offsets_fwd) = lax.scan(
        forward_maps, (identity_w, zero_state), (diag_inv[0], sub_block[0], blocks)
    )
    entering = carried_in(
        (whole_map, whole_shift), "front", compose, (identity_w, zero_state), False
    )
    _, solved_fwd = lax.scan(apply_maps, entering[1], (maps_fwd, offsets_fwd))
    forward_local = solved_fwd.reshape(count * width, columns)
    coupling_full = coupling[0].astype(jnp.float32)
    group_rows = product(coupling_full, forward_local)
    selector = (jnp.arange(S)[:, None] == update_rows[0][None, :]).astype(jnp.float32)
    update_term = product(selector, group_rows)
    gathered = lax.all_gather(sep_inv, "leaf", axis=1, tiled=True)
    whole_inv = lax.all_gather(gathered, "front", axis=0, tiled=True).astype(jnp.float32)
    rows_here = rhs_sep.shape[0]
    placed = lax.dynamic_update_slice_in_dim(
        jnp.zeros((S, columns), jnp.float32), rhs_sep, lax.axis_index("leaf") * rows_here, 0
    )
    leader = (lax.axis_index("front") == 0).astype(jnp.float32)
    reduced = lax.psum(leader * placed - update_term, ("leaf", "front"))
    sep_forward = product(whole_inv, reduced)
    solution_all = product(whole_inv.T, sep_forward)
    solution_sep = lax.dynamic_slice_in_dim(
        solution_all, lax.axis_index("leaf") * rows_here, rows_here, 0
    )
    selected_entries = product(selector.T, solution_all)
    adjusted = forward_local - product(coupling_full.T, selected_entries)
    next_first = shifted_2(sub_block[0, 0], "front", -1)
    following = jnp.concatenate([sub_block[0, 1:], next_first[None]], axis=0)
    adjusted_blocks = adjusted.reshape(count, width, columns)
    (back_map, back_shift), (maps_back, offsets_back) = lax.scan(
        backward_maps,
        (identity_w, zero_state),
        (diag_inv[0], following, adjusted_blocks),
        reverse=True,
    )
    arriving = carried_in((back_map, back_shift), "front", compose, (identity_w, zero_state), True)
    _, solved_back = lax.scan(apply_maps, arriving[1], (maps_back, offsets_back), reverse=True)
    return (solved_back, solution_sep)


def solution(mesh):
    return jax.shard_map(
        shards,
        mesh=mesh,
        in_specs=(
            P("leaf", "front", None),
            P("leaf", "front", None, None),
            P("leaf", "front", None, None),
            P("leaf", None, "front"),
            P("leaf", None),
            P("leaf", None),
            P("front", "leaf"),
        ),
        out_specs=(P("leaf", "front", None), P("leaf", None)),
        check_vma=False,
    )
```

profile of v0, /device:TPU:0, one launch (start us, length us, event | category | flops | bytes accessed | tf_op | source)
XLA Modules:
  0.0 245.7 jit_solution(13124845417316200062)
XLA Ops:
  7.2 0.0 copy-start
  7.2 0.0 all-gather.12.cloned.1.call-start
  7.2 0.8 copy-done
  8.1 1.1 convolution_negate_fusion
  9.2 0.0 copy-start.3
  9.2 1.0 fusion.23
  10.2 0.0 all-gather.12.cloned.1.call-update
  10.2 0.0 all-gather.8.cloned.1.call-start
  10.2 1.3 collective-permute-start
  11.5 17.9 %all_gather.36 = bf16[128,1024]{1,0:T(8,128)(2,1)} all-gather(bf16[128,256]{1,0:T(8,128)(2,1)} %param.17), channel_id=1, replica_groups=mesh['leaf'=4,'front'=8] {'leaf'}, dimensions={1}, use_global_device_ids=true | all-gather | bytes 327680 | tf_op jit(solution)/shard_map/all_gather | solution.py:88
  29.5 0.0 all-gather.8.cloned.1.call-update
  29.5 0.0 all-reduce.2.cloned.1.call-start
  29.5 1.1 fusion.29
  30.7 0.4 convolution_add_fusion.4
  31.0 11.6 %all-gather.2 = f32[2048,64]{0,1:T(8,128)S(1)} all-gather(f32[256,64]{0,1:T(8,128)S(1)} %convolution_add_fusion.4), channel_id=4, replica_groups=mesh['leaf'=4,'front'=8] {'front'}, dimensions={0}, use_global_device_ids=true | all-gather | bytes 589824 | tf_op jit(solution)/shard_map/all_gather | solution.py:14
  42.6 0.2 copy.13
  42.9 0.0 collective-permute-done
  42.9 0.2 convolution_negate_fusion.1
  43.1 0.0 all-gather.12.cloned.1.call-done
  43.1 0.0 copy-start.2
  43.1 0.0 copy-start.4
  43.2 10.0 %while.18 = (s32[]{:T(128)}, f32[256,64]{0,1:T(8,128)S(1)}, s32[]{:T(128)}, f32[8,256,256]{2,1,0:T(8,128)}, f32[8,256,64]{1,0,2:T(8,128)S(1)}, /*index=5*/s32[]{:T(128)}, s32[]{:T(128)}) while((s32[]{:T(128)}, f32[256,64]{0,1:T(8,128)S(1)}, s32[]{:T(128)}, f32[8,256,256]{2,1,0:T(8,128)}, f32[8,256,64]{1,0,2:T(8,128)S(1)}, ...), condition=%wide.region_1.2_spmd.clone, body=%wide.region_0.1_spmd.clone.sunk | while | flops 50397188 | bytes 788587 | solution.py:26
  43.2 0.1 constant_dynamic-slice_fusion.2
  43.3 1.3 fusion.67
  44.6 0.1 constant_dynamic-slice_fusion.2
  44.7 1.3 fusion.67
  46.0 0.1 constant_dynamic-slice_fusion.2
  46.1 1.3 fusion.67
  47.4 0.1 constant_dynamic-slice_fusion.2
  47.5 1.3 fusion.67
  48.9 0.1 constant_dynamic-slice_fusion.2
  48.9 1.3 fusion.67
  50.3 0.1 constant_dynamic-slice_fusion.2
  50.4 1.3 fusion.67
  51.7 0.1 constant_dynamic-slice_fusion.2
  51.8 1.3 fusion.67
  53.1 0.4 convolution_add_fusion.3
  53.5 0.3 fusion.26
  53.8 1.3 convolution_subtract_fusion
  55.1 0.0 all-reduce.2.cloned.1.call-update
  55.2 0.0 all-gather.10.cloned.1.call-start
  55.2 1.0 fusion.24
  56.2 0.0 all-gather.10.cloned.1.call-update
  56.2 16.5 %all-gather.8.cloned.1.call-done = bf16[1024,1024]{1,0:T(8,128)(2,1)} async-done(((bf16[128,1024]{1,0:T(8,128)(2,1)}), bf16[1024,1024]{1,0:T(8,128)(2,1)}) %all-gather.8.cloned.1.call-update) | async-done | bytes 2097168 | tf_op jit(solution)/shard_map/all_gather | solution.py:89
  72.7 130.5 %all-reduce.2.cloned.1.call-done = f32[1024,64]{0,1:T(8,128)} async-done(((f32[1024,64]{0,1:T(8,128)}), f32[1024,64]{0,1:T(8,128)}) %all-reduce.2.cloned.1.call-update) | async-done | bytes 262160 | tf_op jit(solution)/shard_map/psum | solution.py:95
  203.3 3.7 %fusion.39 = f32[64,1024]{1,0:T(8,128)S(1)} fusion(f32[1024,64]{0,1:T(8,128)} %all-reduce.2.cloned.1.call-done, bf16[1024,1024]{1,0:T(8,128)(2,1)} %all-gather.8.cloned.1.call-done), kind=kOutput, calls=%fused_computation.56 | convolution fusion | flops 805306368 | bytes 2621440 | tf_op jit(solution)/shard_map/dot_general | solution.py:36
  207.0 1.2 fusion.40
  208.2 0.7 fusion.19
  208.9 0.3 fusion.16
  209.2 0.2 convolution_bitcast_fusion
  209.4 0.4 convolution_add_fusion.5
  209.8 10.4 %all-gather.3 = f32[2048,64]{0,1:T(8,128)S(1)} all-gather(f32[256,64]{0,1:T(8,128)S(1)} %convolution_add_fusion.5), channel_id=5, replica_groups=mesh['leaf'=4,'front'=8] {'front'}, dimensions={0}, use_global_device_ids=true | all-gather | bytes 589824 | tf_op jit(solution)/shard_map/all_gather | solution.py:14
  220.3 0.6 dynamic-slice_bitcast_fusion
  221.0 12.4 %all-gather.10.cloned.1.call-done = f32[2048,256]{1,0:T(8,128)} async-done(((f32[256,256]{1,0:T(8,128)}), f32[2048,256]{1,0:T(8,128)}) %all-gather.10.cloned.1.call-update) | async-done | bytes 2097168 | tf_op jit(solution)/shard_map/all_gather | solution.py:14
  233.4 1.8 rev.6
  235.2 2.9 %while.19 = (s32[]{:T(128)}, f32[256,64]{0,1:T(8,128)S(1)}, s32[]{:T(128)}, f32[8,256,256]{2,1,0:T(8,128)S(1)}, f32[8,256,64]{1,2,0:T(8,128)S(1)}, /*index=5*/s32[]{:T(128)}, s32[]{:T(128)}) while((s32[]{:T(128)}, f32[256,64]{0,1:T(8,128)S(1)}, s32[]{:T(128)}, f32[8,256,256]{2,1,0:T(8,128)S(1)}, f32[8,256,64]{1,2,0:T(8,128)S(1)}, ...), condition=%wide.region_4.5_spmd.clone, body=%wide.region_3.4_spmd.clone.sunk | while | flops 50397188 | bytes 658023 | solution.py:26
  235.3 0.4 fusion.70
  235.7 0.4 fusion.70
  236.1 0.4 fusion.70
  236.5 0.4 fusion.70
  236.9 0.4 fusion.70
  237.3 0.4 fusion.70
  237.8 0.4 fusion.70
  238.1 1.0 fusion.17
  (25 shorter events, 0.2 us)
Async XLA Ops:
  7.2 0.9 copy-start
  7.2 35.9 %all-gather.12.cloned.1.call-start = ((), (), s32[]{:S(2)}) async-start(), calls=%async_computation.3 | async-start | bytes 2359296 | tf_op jit(solution)/shard_map/all_gather | solution.py:14
  9.2 33.7 %copy-start.3 = (f32[256,64]{0,1:T(8,128)S(1)}, f32[256,64]{0,1:T(8,128)}, u32[]{:S(2)}) copy-start(f32[256,64]{0,1:T(8,128)} %param.16) | copy-start | bytes 196612
  10.2 62.6 %all-gather.8.cloned.1.call-start = ((), (), s32[]{:S(2)}) async-start(), calls=%async_computation.1 | async-start | bytes 2359296 | tf_op jit(solution)/shard_map/all_gather | solution.py:89
  10.2 32.6 %collective-permute-start = (bf16[256,256]{1,0:T(8,128)(2,1)}, bf16[256,256]{1,0:T(8,128)(2,1)S(1)}, u32[]{:S(2)}, u32[]{:S(2)}) collective-permute-start(bf16[256,256]{1,0:T(8,128)(2,1)} %bitcast.85), channel_id=1, source_target_pairs={{1,0},{2,1},{3,2},{4,3},{5,4},{6,5},{7,6},{9,8},{10,9},{11,10},{12... | collective-permute-start | bytes 393224 | tf_op jit(solution)/shard_map/ppermute | solution.py:32
  29.5 173.8 %all-reduce.2.cloned.1.call-start = ((), (), s32[]{:S(2)}) async-start(), calls=%async_computation | async-start | bytes 524288 | tf_op jit(solution)/shard_map/psum | solution.py:95
  43.1 10.4 %copy-start.2 = (bf16[1,256,256]{2,1,0:T(8,128)(2,1)S(1)}, bf16[1,256,256]{2,1,0:T(8,128)(2,1)}, u32[]{:S(2)}) copy-start(bf16[1,256,256]{2,1,0:T(8,128)(2,1)} %param.14) | copy-start | bytes 393220
  43.1 10.6 %copy-start.4 = (s32[1,256]{1,0:T(1,128)S(1)}, s32[1,256]{1,0:T(1,128)}, u32[]{:S(2)}) copy-start(s32[1,256]{1,0:T(1,128)} %param.15) | copy-start | bytes 3076
  55.2 178.2 %all-gather.10.cloned.1.call-start = ((), (), s32[]{:S(2)}) async-start(), calls=%async_computation.2 | async-start | bytes 2359296 | tf_op jit(solution)/shard_map/all_gather | solution.py:14
  72.7 134.2 %copy-start.1 = (bf16[1024,1024]{1,0:T(8,128)(2,1)S(1)}, bf16[1024,1024]{1,0:T(8,128)(2,1)}, u32[]{:S(2)}) copy-start(bf16[1024,1024]{1,0:T(8,128)(2,1)} %all-gather.8.cloned.1.call-done) | copy-start | bytes 6291460
Sparse Core Ops, SparseCore 0:
  10.3 31.7 all-gather.11
  44.0 28.7 all-gather.7
  78.2 124.9 all-reduce.1
  205.0 28.3 all-gather.9
where the time goes:
time: 246 us
  waiting for transfers between devices  160 us (65%)
  blocking collectives  40 us (16%)
  matrix products  26.2 us (11%)
  between operations  14 us (6%)
  local copies, waits for them, and re-layouts  4.04 us (2%)
    psum x1, waiting for transfers between devices, shards(): reduced = lax.psum(leader * placed - update_term, ('leaf', 'front'))  131 us
    dot_general x28, matrix products, product(): return jnp.matmul(left, right, precision=PRECISE)  24.9 us
    all_gather x2, blocking collectives, carried_in(): pieces = jax.tree.map(lambda part: lax.all_gather(part, axis), value)  22 us
    all_gather x1, blocking collectives, shards(): gathered = lax.all_gather(sep_inv, 'leaf', axis=1, tiled=True)  17.9 us
    all_gather x1, waiting for transfers between devices, shards(): lax.all_gather(gathered, 'front', axis=0, tiled=True).astype(jnp.float32)  16.5 us
    all_gather x2, waiting for transfers between devices, carried_in(): pieces = jax.tree.map(lambda part: lax.all_gather(part, axis), value)  12.5 us
  transfers between devices with their start and end apart: 5, of which 3 were waited for; matrix products, arithmetic and copies ran while one was open for 9% of the time, Pallas kernels for 0%

commit v1 on v0

v1 whole, which is shorter than its diff:
```python
import functools

import jax
import jax.numpy as jnp
from jax import lax
from jax.experimental import pallas as pl
from jax.experimental.pallas import tpu as pltpu
from jax.sharding import PartitionSpec as P

MESH = pl.DeviceIdType.MESH
F32 = jnp.float32
BF16 = jnp.bfloat16


def halves(x):
    head = x.astype(BF16)
    rest = (x - head.astype(F32)).astype(BF16)
    return jnp.concatenate([head, rest], axis=0)


def joined(both):
    rows = both.shape[0] // 2
    return both[:rows] + both[rows:]


def times(x, w):
    return joined(jnp.dot(halves(x), w, preferred_element_type=F32))


def times_t(x, w):
    dims = (((1,), (1,)), ((), ()))
    return joined(lax.dot_general(halves(x), w, dims, preferred_element_type=F32))


def kernel(
    groups, chips, skips,
    r_ref, d_ref, b_ref, c_ref, idx_ref, rs_ref, sp_ref,
    out_ref, sol_ref,
    fac, rt, rbuf, ybuf, yin, uin, uout, ubuf, rst, rsbuf, idxbuf, sepbuf, sel, ssep, solt,
    zbuf, solbuf, vin, vout, xs, obuf,
    loc_s, swap_s, swap_r, y_s, y_r, u_s, u_r, v_s, v_r,
    ux_s, ux_r, rs_s, rs_r, id_s, id_r, sep_s, sep_r, fwd_s, fwd_r,
    z_s, z_r, so_s, so_r, x_s, x_r, sx_s, sx_r,
):
    plane = lax.axis_index("leaf")
    front = lax.axis_index("front")
    chip = front // 2
    core = front % 2
    other = 1 - core
    last = chips - 1
    is_last = chip == last
    sibling = (plane, chip * 2 + other)
    half = rbuf.shape[1]
    wide = solt.shape[1] // groups
    deep = sepbuf.shape[3]

    def remote(src, dst, send, recv, to):
        return pltpu.make_async_remote_copy(
            src_ref=src, dst_ref=dst, send_sem=send, recv_sem=recv, device_id=to, device_id_type=MESH
        )

    barrier = pltpu.get_barrier_semaphore()

    def greet(to):
        pl.semaphore_signal(barrier, inc=1, device_id=to, device_id_type=MESH)

    greet(sibling)

    @pl.when(is_last)
    def _():
        for g in range(groups):
            for c in range(chips):
                if c < last:
                    greet((g, c * 2 + core))
                else:
                    @pl.when(plane != g)
                    def _(g=g, c=c):
                        greet((g, c * 2 + core))

    @pl.when(jnp.logical_not(is_last))
    def _():
        for g in range(groups):
            greet((g, last * 2 + core))

        @pl.when(chip > 0)
        def _():
            greet((plane, front - 2))

        @pl.when(chip + 1 < last)
        def _():
            greet((plane, front + 2))

    near = (chip > 0).astype(jnp.int32) + (chip + 1 < last).astype(jnp.int32)
    pl.semaphore_wait(barrier, jnp.where(is_last, groups * chips, groups + 1 + near))

    swaps = []
    locals_ = []
    for i, ref in enumerate((b_ref, d_ref, c_ref)):
        copy = remote(ref, fac.at[i, core], swap_s.at[i], swap_r.at[i], sibling)
        copy.start()
        swaps.append(copy)
        copy = pltpu.make_async_copy(ref, fac.at[i, core], loc_s.at[i])
        copy.start()
        locals_.append(copy)
    flipped = r_ref[...].T
    rt[0] = flipped[:half]
    rt[1] = flipped[half:]
    rbuf[core] = rt[core]
    copy = remote(rt.at[other], rbuf.at[core], swap_s.at[3], swap_r.at[3], sibling)
    copy.start()
    swaps.append(copy)

    def sep_copies(g):
        return remote(
            sp_ref, sepbuf.at[plane, core, chip], sep_s.at[g], sep_r.at[plane], (g, last * 2 + core)
        )

    useful = chip >= (plane * wide) // (2 * deep)
    for g in range(groups):
        mine = jnp.logical_and(is_last, plane == g)

        @pl.when(jnp.logical_and(useful, jnp.logical_not(mine)))
        def _(g=g):
            sep_copies(g).start()

        @pl.when(mine)
        def _(g=g):
            pltpu.make_async_copy(sp_ref, sepbuf.at[g, core, last], sep_r.at[g]).start()

    def peers(action):
        for g in range(groups):
            @pl.when(plane != g)
            def _(g=g):
                action(g, (g, last * 2 + core))

    @pl.when(is_last)
    def _():
        upright = rs_ref[...].T
        rst[0] = upright[:half]
        rst[1] = upright[half:]
        rsbuf[plane] = rst[core]
        idxbuf[plane] = idx_ref[...]

        def give(g, to):
            remote(rst.at[core], rsbuf.at[plane], rs_s.at[g], rs_r.at[plane], to).start()
            remote(idx_ref, idxbuf.at[plane], id_s.at[g], id_r.at[plane], to).start()

        peers(give)

    for copy in locals_:
        copy.wait()
    for copy in swaps:
        copy.wait_recv()

    @pl.when(is_last)
    def _():
        def take(g, to):
            remote(idx_ref, idxbuf.at[g], id_s.at[g], id_r.at[g], to).wait_recv()
            remote(rst.at[core], rsbuf.at[g], rs_s.at[g], rs_r.at[g], to).wait_recv()

        peers(take)
        for g in range(groups):
            rows = lax.broadcasted_iota(jnp.int32, sel.shape[1:], 0)
            sel[g] = (rows == idxbuf[g]).astype(F32).astype(BF16)
        for g in range(groups):
            part = sepbuf.at[g, core, pl.ds(skips[g], chips - skips[g])]
            pltpu.make_async_copy(part, part, sep_r.at[g]).wait()
            remote(part, part, fwd_s.at[g], fwd_r.at[g], sibling).start()

    @pl.when(chip == 0)
    def _():
        yin[...] = jnp.zeros_like(yin)
        uin[...] = jnp.zeros_like(uin)

    onward = (plane, jnp.minimum(front + 2, last * 2 + core))
    behind = (plane, jnp.maximum(front - 2, core))
    y_copy = remote(ybuf.at[1], yin, y_s, y_r, onward)
    u_copy = remote(uout, uin, u_s, u_r, onward)

    @pl.when(chip > 0)
    def _():
        y_copy.wait_recv()

    first = times_t(rbuf[0] - times_t(yin[...], fac[0, 0]), fac[1, 0])
    second = times_t(rbuf[1] - times_t(first, fac[0, 1]), fac[1, 1])
    ybuf[0] = first
    ybuf[1] = second

    @pl.when(jnp.logical_not(is_last))
    def _():
        y_copy.start()

    update = times_t(first, fac[2, 0]) + times_t(second, fac[2, 1])

    @pl.when(chip > 0)
    def _():
        u_copy.wait_recv()

    uout[...] = update + uin[...]

    @pl.when(jnp.logical_not(is_last))
    def _():
        u_copy.start()

    z_copies = [
        remote(zbuf, zbuf, z_s.at[c], z_r, (plane, c * 2 + core)) for c in range(last)
    ]
    so_copies = [
        remote(solbuf.at[core], solbuf.at[core], so_s.at[c], so_r, (plane, c * 2 + core))
        for c in range(last)
    ]

    @pl.when(is_last)
    def _():
        ubuf[plane] = uout[...]
        peers(lambda g, to: remote(uout, ubuf.at[plane], ux_s.at[g], ux_r.at[plane], to).start())
        for g in range(groups):
            part = sepbuf.at[g, other, pl.ds(skips[g], chips - skips[g])]
            remote(part, part, fwd_s.at[g], fwd_r.at[g], sibling).wait_recv()
        peers(lambda g, to: remote(uout, ubuf.at[g], ux_s.at[g], ux_r.at[g], to).wait_recv())
        total = times_t(ubuf[0], sel[0])
        for g in range(1, groups):
            total = total + times_t(ubuf[g], sel[g])
        ssep[...] = jnp.zeros_like(ssep)
        for g in range(groups):
            part = halves(rsbuf[g] - total[:, g * wide : (g + 1) * wide])
            for k in range(2):
                block = sepbuf[g, k, skips[g] :].reshape((chips - skips[g]) * deep, wide)
                ssep[k, :, skips[g] * deep :] += joined(
                    lax.dot_general(part, block, (((1,), (1,)), ((), ())), preferred_element_type=F32)
                )
        for g in range(groups):
            part = 0
            for k in range(2):
                block = sepbuf[g, k, skips[g] :].reshape((chips - skips[g]) * deep, wide)
                part = part + times(ssep[k, :, skips[g] * deep :], block)
            solt[:, g * wide : (g + 1) * wide] = part

            @pl.when(plane == g)
            def _(part=part):
                solbuf[core] = part

        zbuf[...] = times(solt[...], sel[plane])
        for copy in reversed(z_copies):
            copy.start()
        for copy in so_copies:
            copy.start()

    @pl.when(jnp.logical_not(is_last))
    def _():
        z_copies[0].wait_recv()

    picked = halves(zbuf[...])
    a_first = ybuf[0] - joined(jnp.dot(picked, fac[2, 0], preferred_element_type=F32))
    a_second = ybuf[1] - joined(jnp.dot(picked, fac[2, 1], preferred_element_type=F32))
    v_copy = remote(vout, vin, v_s, v_r, behind)

    @pl.when(is_last)
    def _():
        vin[...] = jnp.zeros_like(vin)

    @pl.when(jnp.logical_not(is_last))
    def _():
        v_copy.wait_recv()

    x_second = times(a_second - vin[...], fac[1, 1])
    x_first = times(a_first - times(x_second, fac[0, 1]), fac[1, 0])

    @pl.when(chip > 0)
    def _():
        vout[...] = times(x_first, fac[0, 0])
        v_copy.start()

    xs[0] = x_first
    xs[1] = x_second
    obuf[core] = xs[core]
    x_copy = remote(xs.at[other], obuf.at[core], x_s, x_r, sibling)
    x_copy.start()

    @pl.when(jnp.logical_not(is_last))
    def _():
        so_copies[0].wait_recv()

    sx_copy = remote(solbuf.at[core], solbuf.at[core], sx_s, sx_r, sibling)
    sx_copy.start()
    x_copy.wait_recv()
    for k in range(2):
        out_ref[k * half : (k + 1) * half] = obuf[k]
    sx_copy.wait_recv()
    for k in range(2):
        sol_ref[k * half : (k + 1) * half] = solbuf[k]

    for copy in swaps:
        copy.wait_send()
    for g in range(groups):
        mine = jnp.logical_and(is_last, plane == g)

        @pl.when(jnp.logical_and(useful, jnp.logical_not(mine)))
        def _(g=g):
            sep_copies(g).wait_send()

    @pl.when(jnp.logical_not(is_last))
    def _():
        y_copy.wait_send()
        u_copy.wait_send()

    @pl.when(chip > 0)
    def _():
        v_copy.wait_send()

    @pl.when(is_last)
    def _():
        def sent(g, to):
            remote(rst.at[core], rsbuf.at[plane], rs_s.at[g], rs_r.at[plane], to).wait_send()
            remote(idx_ref, idxbuf.at[plane], id_s.at[g], id_r.at[plane], to).wait_send()
            remote(uout, ubuf.at[plane], ux_s.at[g], ux_r.at[plane], to).wait_send()

        peers(sent)
        for g in range(groups):
            part = sepbuf.at[g, core, pl.ds(skips[g], chips - skips[g])]
            remote(part, part, fwd_s.at[g], fwd_r.at[g], sibling).wait_send()
        for copy in z_copies:
            copy.wait_send()
        for copy in so_copies:
            copy.wait_send()

    x_copy.wait_send()
    sx_copy.wait_send()


def solution(mesh):
    groups, fronts = mesh.shape["leaf"], mesh.shape["front"]
    chips = fronts // 2

    def shards(rhs_leaf, diag_inv, sub_block, coupling, update_rows, rhs_sep, sep_inv):
        width, columns = rhs_leaf.shape[1:]
        picks = coupling.shape[1]
        wide = rhs_sep.shape[0]
        deep = sep_inv.shape[0]
        rows = wide * groups
        half = columns // 2
        skips = tuple(g * wide // (2 * deep) for g in range(groups))
        vmem = pl.BlockSpec(memory_space=pltpu.VMEM)
        anywhere = pl.BlockSpec(memory_space=pl.ANY)
        dma = pltpu.SemaphoreType.DMA
        out, sol = pl.pallas_call(
            functools.partial(kernel, groups, chips, skips),
            out_shape=(
                jax.ShapeDtypeStruct((columns, width), F32),
                jax.ShapeDtypeStruct((columns, wide), F32),
            ),
            in_specs=[vmem, anywhere, anywhere, anywhere, vmem, vmem, anywhere],
            out_specs=(vmem, vmem),
            scratch_shapes=[
                pltpu.VMEM((3, 2, width, width), BF16),
                pltpu.VMEM((2, half, width), F32),
                pltpu.VMEM((2, half, width), F32),
                pltpu.VMEM((2, half, width), F32),
                pltpu.VMEM((half, width), F32),
                pltpu.VMEM((half, picks), F32),
                pltpu.VMEM((half, picks), F32),
                pltpu.VMEM((groups, half, picks), F32),
                pltpu.VMEM((2, half, wide), F32),
                pltpu.VMEM((groups, half, wide), F32),
                pltpu.VMEM((groups, 1, picks), jnp.int32),
                pltpu.VMEM((groups, 2, chips, deep, wide), BF16),
                pltpu.VMEM((groups, rows, picks), BF16),
                pltpu.VMEM((2, half, chips * deep), F32),
                pltpu.VMEM((half, rows), F32),
                pltpu.VMEM((half, picks), F32),
                pltpu.VMEM((2, half, wide), F32),
                pltpu.VMEM((half, width), F32),
                pltpu.VMEM((half, width), F32),
                pltpu.VMEM((2, half, width), F32),
                pltpu.VMEM((2, half, width), F32),
                dma((3,)), dma((4,)), dma((4,)), dma, dma, dma, dma, dma, dma,
                dma((groups,)), dma((groups,)), dma((groups,)), dma((groups,)),
                dma((groups,)), dma((groups,)), dma((groups,)), dma((groups,)),
                dma((groups,)), dma((groups,)),
                dma((chips,)), dma, dma((chips,)), dma, dma, dma, dma, dma,
            ],
            compiler_params=pltpu.CompilerParams(
                collective_id=0, has_side_effects=True, vmem_limit_bytes=40 * 1024 * 1024
            ),
        )(
            rhs_leaf[0], diag_inv[0, 0], sub_block[0, 0], coupling[0],
            update_rows, rhs_sep, sep_inv,
        )
        return out.T[None], sol.T

    return jax.shard_map(
        shards,
        mesh=mesh,
        in_specs=(
            P("leaf", "front", None),
            P("leaf", "front", None, None),
            P("leaf", "front", None, None),
            P("leaf", None, "front"),
            P("leaf", None),
            P("leaf", None),
            P("front", "leaf"),
        ),
        out_specs=(P("leaf", "front", None), P("leaf", None)),
        check_vma=False,
    )
```

time: 246 us -> 44 us (0.18)
  waiting for transfers between devices: 160 us -> 0 us
  blocking collectives: 40 us -> 0 us
  Pallas kernels: 0 us -> 39 us
  matrix products: 26.2 us -> 0 us
  between operations: 14 us -> 0.72 us
    psum x1 -> x0, waiting for transfers between devices: 131 us -> none  [shards(): reduced = lax.psum(leader * placed - update_term, ('leaf', 'front'))]
    all_gather x3 -> x0, blocking collectives: 40 us -> none  [the longest x2 22 us: carried_in(): pieces = jax.tree.map(lambda part: lax.all_gather(part, axis), value)]
    pallas_call x0 -> x1, Pallas kernels: none -> 39 us  [shards(): pl.pallas_call(functools.partial(kernel, groups, chips, skips), out_shape...]
    all_gather x3 -> x0, waiting for transfers between devices: 29 us -> none  [the longest x1 16.5 us: shards(): lax.all_gather(gathered, 'front', axis=0, tiled=True).astype(jnp.float32)]
    dot_general x30 -> x0, matrix products: 26.2 us -> none  [the longest x28 24.9 us: product(): return jnp.matmul(left, right, precision=PRECISE)]
    unnamed x11 -> x14, local copies, waits for them, and re-layouts: 1.04 us -> 4.06 us
  transfers between devices with their start and end apart: 5 -> 0, of which waited for: 3 -> 0; matrix products, arithmetic and copies ran while one was open for 9% -> 0% of each run, Pallas kernels for 0% -> 0%
where the time goes in v1:
time: 44 us; the launch traced here: 43.8 us
  Pallas kernels  39 us (89%)
  local copies, waits for them, and re-layouts  4.06 us (9%)
  between operations  0.72 us (2%)
    pallas_call x1, Pallas kernels, shards(): pl.pallas_call(functools.partial(kernel, groups, chips, skips), out_shape...  39 us
    unnamed x14, local copies, waits for them, and re-layouts  4.06 us

profile of v1, /device:TPU:0, one launch (start us, length us, event | category | flops | bytes accessed | tf_op | source)
XLA Modules:
  0.0 43.8 jit_solution(2699804347504395459)
XLA Ops:
  0.6 0.0 copy-start.1
  0.6 0.0 copy-start.2
  0.6 1.0 %copy.9 = f32[1,256,64]{2,1,0:T(8,128)S(1)} copy(f32[1,256,64]{1,2,0:T(8,128)} %param.7) | data formatting | bytes 131072 | tf_op args[0]
  1.6 0.0 copy-start
  1.6 0.0 copy-start.4
  1.7 1.0 %copy.10.rs_ref = f32[256,64]{1,0:T(8,128)S(1)} copy(f32[256,64]{0,1:T(8,128)} %param.12) | data formatting | bytes 131072 | tf_op args[5]
  2.6 0.0 copy-done.1
  2.6 0.0 copy-done.2
  2.6 0.0 copy-done
  2.7 0.0 copy-done.4
  2.7 0.0 copy-start.3
  2.7 0.8 %copy-done.3 = bf16[128,256]{1,0:T(8,128)(2,1)S(1)} copy-done((bf16[128,256]{1,0:T(8,128)(2,1)S(1)}, bf16[128,256]{1,0:T(8,128)(2,1)}, u32[]{:S(2)}) %copy-start.3) | copy-done | bytes 65560
  3.5 39.0 %shard_map.86 = (f32[64,256]{1,0:T(8,128)S(1)}, f32[64,256]{1,0:T(8,128)S(1)}) custom-call(f32[256,64]{1,0:T(8,128)S(1)} %bitcast.8, bf16[256,256]{1,0:T(8,128)(2,1)S(1)} %bitcast.9, bf16[256,256]{1,0:T(8,128)(2,1)S(1)} %bitcast.10, bf16[256,256]{1,0:T(8,128)(2,1)S(1)} %bitcast.11, s32[1,256]{1,0:T(1,128)S(1)} %copy-done.4, f32[256,64]{1,0:T(8,128)S(1)} %copy.10.rs_ref, ...), custom_call_target="tpu_custom_call" | custom-call | tf_op jit(solution)/shard_map/pallas_call | solution.py:346
  42.5 0.6 %copy.13 = f32[1,256,64]{1,2,0:T(8,128)} copy(f32[1,256,64]{1,2,0:T(8,128)S(1)} %bitcast.13) | data formatting | bytes 131072
  43.2 0.6 %copy.14 = f32[256,64]{0,1:T(8,128)} copy(f32[256,64]{0,1:T(8,128)S(1)} %bitcast.12) | data formatting | bytes 131072
Async XLA Ops:
  0.6 2.0 %copy-start.1 = (bf16[1,1,256,256]{3,2,1,0:T(8,128)(2,1)S(1)}, bf16[1,1,256,256]{3,2,1,0:T(8,128)(2,1)}, u32[]{:S(2)}) copy-start(bf16[1,1,256,256]{3,2,1,0:T(8,128)(2,1)} %param.9) | copy-start | bytes 393220
  0.6 2.0 %copy-start.2 = (bf16[1,256,256]{2,1,0:T(8,128)(2,1)S(1)}, bf16[1,256,256]{2,1,0:T(8,128)(2,1)}, u32[]{:S(2)}) copy-start(bf16[1,256,256]{2,1,0:T(8,128)(2,1)} %param.10) | copy-start | bytes 393220
  1.6 1.0 %copy-start = (bf16[1,1,256,256]{3,2,1,0:T(8,128)(2,1)S(1)}, bf16[1,1,256,256]{3,2,1,0:T(8,128)(2,1)}, u32[]{:S(2)}) copy-start(bf16[1,1,256,256]{3,2,1,0:T(8,128)(2,1)} %param.8) | copy-start | bytes 393220
  1.6 1.0 %copy-start.4 = (s32[1,256]{1,0:T(1,128)S(1)}, s32[1,256]{1,0:T(1,128)}, u32[]{:S(2)}) copy-start(s32[1,256]{1,0:T(1,128)} %idx_ref.1) | copy-start | bytes 3076
  2.7 0.8 %copy-start.3 = (bf16[128,256]{1,0:T(8,128)(2,1)S(1)}, bf16[128,256]{1,0:T(8,128)(2,1)}, u32[]{:S(2)}) copy-start(bf16[128,256]{1,0:T(8,128)(2,1)} %sp_ref.1) | copy-start | bytes 196612

commit v2 on v1

--- a/solution.py
+++ b/solution.py
@@ -32,11 +32,29 @@
     return joined(lax.dot_general(halves(x), w, dims, preferred_element_type=F32))
 
 
+def dot(a, b):
+    return jnp.dot(a, b, preferred_element_type=F32)
+
+
+def dot_t(a, b):
+    return lax.dot_general(a, b, (((1,), (1,)), ((), ())), preferred_element_type=F32)
+
+
+def split(x):
+    head = x.astype(BF16)
+    return head, (x - head.astype(F32)).astype(BF16)
+
+
+def through(x, w, multiply):
+    both = halves(x)
+    return joined(multiply(both, w[0])) + multiply(both[: x.shape[0]], w[1])
+
+
 def kernel(
     groups, chips, skips,
     r_ref, d_ref, b_ref, c_ref, idx_ref, rs_ref, sp_ref,
     out_ref, sol_ref,
-    fac, rt, rbuf, ybuf, yin, uin, uout, ubuf, rst, rsbuf, idxbuf, sepbuf, sel, ssep, solt,
+    fac, gmap, hmap, rbuf, ybuf, yin, uin, uout, ubuf, rsbuf, idxbuf, sepbuf, sel, ssep, solt,
     zbuf, solbuf, vin, vout, xs, obuf,
     loc_s, swap_s, swap_r, y_s, y_r, u_s, u_r, v_s, v_r,
     ux_s, ux_r, rs_s, rs_r, id_s, id_r, sep_s, sep_r, fwd_s, fwd_r,
@@ -102,11 +120,10 @@
         copy = pltpu.make_async_copy(ref, fac.at[i, core], loc_s.at[i])
         copy.start()
         locals_.append(copy)
-    flipped = r_ref[...].T
-    rt[0] = flipped[:half]
-    rt[1] = flipped[half:]
-    rbuf[core] = rt[core]
-    copy = remote(rt.at[other], rbuf.at[core], swap_s.at[3], swap_r.at[3], sibling)
+    mine_rows = pl.ds(pl.multiple_of(core * half, half), half)
+    other_rows = pl.ds(pl.multiple_of(other * half, half), half)
+    rbuf[core] = r_ref[mine_rows]
+    copy = remote(r_ref.at[other_rows], rbuf.at[core], swap_s.at[3], swap_r.at[3], sibling)
     copy.start()
     swaps.append(copy)
 
@@ -135,14 +152,11 @@
 
     @pl.when(is_last)
     def _():
-        upright = rs_ref[...].T
-        rst[0] = upright[:half]
-        rst[1] = upright[half:]
-        rsbuf[plane] = rst[core]
+        rsbuf[plane] = rs_ref[mine_rows]
         idxbuf[plane] = idx_ref[...]
 
         def give(g, to):
-            remote(rst.at[core], rsbuf.at[plane], rs_s.at[g], rs_r.at[plane], to).start()
+            remote(rs_ref.at[mine_rows], rsbuf.at[plane], rs_s.at[g], rs_r.at[plane], to).start()
             remote(idx_ref, idxbuf.at[plane], id_s.at[g], id_r.at[plane], to).start()
 
         peers(give)
@@ -152,11 +166,43 @@
     for copy in swaps:
         copy.wait_recv()
 
+    onward = (plane, jnp.minimum(front + 2, last * 2 + core))
+    behind = (plane, jnp.maximum(front - 2, core))
+    y_copy = remote(ybuf.at[2], yin, y_s, y_r, onward)
+    u_copy = remote(uout, uin, u_s, u_r, onward)
+    u_copies = []
+    for step in range(1, groups):
+        g = lax.rem(plane + step, groups)
+        u_copies.append(
+            remote(uout, ubuf.at[plane], ux_s.at[step - 1], ux_r.at[plane], (g, last * 2 + core))
+        )
+
+    own_first = times_t(rbuf[0], fac[1, 0])
+    own_second = times_t(rbuf[1] - times_t(own_first, fac[0, 1]), fac[1, 1])
+
+    @pl.when(chip == 0)
+    def _():
+        yin[...] = jnp.zeros_like(yin)
+        uin[...] = jnp.zeros_like(uin)
+        ybuf[2] = own_second
+        y_copy.start()
+
+    own_update = times_t(own_first, fac[2, 0]) + times_t(own_second, fac[2, 1])
+    early = split(dot(fac[1, 0], fac[0, 0]))
+    late = split(dot(fac[1, 1], fac[0, 1]))
+    whole = split(dot(late[0], early[0]) + (dot(late[1], early[0]) + dot(late[0], early[1])))
+    gmap[0], gmap[1] = whole
+    seen = split(
+        dot(fac[2, 1], whole[0]) - dot(fac[2, 0], early[0])
+        + (dot(fac[2, 1], whole[1]) - dot(fac[2, 0], early[1]))
+    )
+    hmap[0], hmap[1] = seen
+
     @pl.when(is_last)
     def _():
         def take(g, to):
             remote(idx_ref, idxbuf.at[g], id_s.at[g], id_r.at[g], to).wait_recv()
-            remote(rst.at[core], rsbuf.at[g], rs_s.at[g], rs_r.at[g], to).wait_recv()
+            remote(rs_ref.at[mine_rows], rsbuf.at[g], rs_s.at[g], rs_r.at[g], to).wait_recv()
 
         peers(take)
         for g in range(groups):
@@ -167,40 +213,39 @@
             pltpu.make_async_copy(part, part, sep_r.at[g]).wait()
             remote(part, part, fwd_s.at[g], fwd_r.at[g], sibling).start()
 
-    @pl.when(chip == 0)
-    def _():
-        yin[...] = jnp.zeros_like(yin)
-        uin[...] = jnp.zeros_like(uin)
-
-    onward = (plane, jnp.minimum(front + 2, last * 2 + core))
-    behind = (plane, jnp.maximum(front - 2, core))
-    y_copy = remote(ybuf.at[1], yin, y_s, y_r, onward)
-    u_copy = remote(uout, uin, u_s, u_r, onward)
-
     @pl.when(chip > 0)
     def _():
         y_copy.wait_recv()
 
-    first = times_t(rbuf[0] - times_t(yin[...], fac[0, 0]), fac[1, 0])
-    second = times_t(rbuf[1] - times_t(first, fac[0, 1]), fac[1, 1])
+    heard = yin[...]
+    second = own_second + through(heard, gmap, dot_t)
+    ybuf[1] = second
+
+    @pl.when(jnp.logical_and(chip > 0, jnp.logical_not(is_last)))
+    def _():
+        ybuf[2] = second
+        y_copy.start()
+
+    update = own_update + through(heard, hmap, dot_t)
+
+    @pl.when(chip > 0)
+    def _():
+        u_copy.wait_recv()
+
+    uout[...] = update + uin[...]
+
+    @pl.when(jnp.logical_not(is_last))
+    def _():
+        u_copy.start()
+
+    @pl.when(is_last)
+    def _():
+        for step in range(1, groups):
+            u_copies[step - 1].start()
+
+    first = own_first - times_t(times_t(heard, fac[0, 0]), fac[1, 0])
     ybuf[0] = first
-    ybuf[1] = second
-
-    @pl.when(jnp.logical_not(is_last))
-    def _():
-        y_copy.start()
-
-    update = times_t(first, fac[2, 0]) + times_t(second, fac[2, 1])
-
-    @pl.when(chip > 0)
-    def _():
-        u_copy.wait_recv()
-
-    uout[...] = update + uin[...]
-
-    @pl.when(jnp.logical_not(is_last))
-    def _():
-        u_copy.start()
+    turned = times(times(first, fac[1, 0]), fac[0, 0]) - through(second, gmap, dot)
 
     z_copies = [
         remote(zbuf, zbuf, z_s.at[c], z_r, (plane, c * 2 + core)) for c in range(last)
@@ -212,14 +257,13 @@
 
     @pl.when(is_last)
     def _():
-        ubuf[plane] = uout[...]
-        peers(lambda g, to: remote(uout, ubuf.at[plane], ux_s.at[g], ux_r.at[plane], to).start())
+        total = times_t(uout[...], sel[plane])
         for g in range(groups):
             part = sepbuf.at[g, other, pl.ds(skips[g], chips - skips[g])]
             remote(part, part, fwd_s.at[g], fwd_r.at[g], sibling).wait_recv()
-        peers(lambda g, to: remote(uout, ubuf.at[g], ux_s.at[g], ux_r.at[g], to).wait_recv())
-        total = times_t(ubuf[0], sel[0])
-        for g in range(1, groups):
+        for step in range(1, groups):
+            g = lax.rem(plane + step, groups)
+            remote(uout, ubuf.at[g], ux_s.at[step - 1], ux_r.at[g], (g, last * 2 + core)).wait_recv()
             total = total + times_t(ubuf[g], sel[g])
         ssep[...] = jnp.zeros_like(ssep)
         for g in range(groups):
@@ -254,23 +298,24 @@
     a_first = ybuf[0] - joined(jnp.dot(picked, fac[2, 0], preferred_element_type=F32))
     a_second = ybuf[1] - joined(jnp.dot(picked, fac[2, 1], preferred_element_type=F32))
     v_copy = remote(vout, vin, v_s, v_r, behind)
+    turned = turned + through(zbuf[...], hmap, dot)
 
     @pl.when(is_last)
     def _():
         vin[...] = jnp.zeros_like(vin)
+        vout[...] = turned
 
     @pl.when(jnp.logical_not(is_last))
     def _():
         v_copy.wait_recv()
+        vout[...] = turned + through(vin[...], gmap, dot)
+
+    @pl.when(chip > 0)
+    def _():
+        v_copy.start()
 
     x_second = times(a_second - vin[...], fac[1, 1])
     x_first = times(a_first - times(x_second, fac[0, 1]), fac[1, 0])
-
-    @pl.when(chip > 0)
-    def _():
-        vout[...] = times(x_first, fac[0, 0])
-        v_copy.start()
-
     xs[0] = x_first
     xs[1] = x_second
     obuf[core] = xs[core]
@@ -311,11 +356,12 @@
     @pl.when(is_last)
     def _():
         def sent(g, to):
-            remote(rst.at[core], rsbuf.at[plane], rs_s.at[g], rs_r.at[plane], to).wait_send()
+            remote(rs_ref.at[mine_rows], rsbuf.at[plane], rs_s.at[g], rs_r.at[plane], to).wait_send()
             remote(idx_ref, idxbuf.at[plane], id_s.at[g], id_r.at[plane], to).wait_send()
-            remote(uout, ubuf.at[plane], ux_s.at[g], ux_r.at[plane], to).wait_send()
 
         peers(sent)
+        for copy in u_copies:
+            copy.wait_send()
         for g in range(groups):
             part = sepbuf.at[g, core, pl.ds(skips[g], chips - skips[g])]
             remote(part, part, fwd_s.at[g], fwd_r.at[g], sibling).wait_send()
@@ -353,14 +399,14 @@
             out_specs=(vmem, vmem),
             scratch_shapes=[
                 pltpu.VMEM((3, 2, width, width), BF16),
+                pltpu.VMEM((2, width, width), BF16),
+                pltpu.VMEM((2, picks, width), BF16),
                 pltpu.VMEM((2, half, width), F32),
-                pltpu.VMEM((2, half, width), F32),
-                pltpu.VMEM((2, half, width), F32),
+                pltpu.VMEM((3, half, width), F32),
                 pltpu.VMEM((half, width), F32),
                 pltpu.VMEM((half, picks), F32),
                 pltpu.VMEM((half, picks), F32),
                 pltpu.VMEM((groups, half, picks), F32),
-                pltpu.VMEM((2, half, wide), F32),
                 pltpu.VMEM((groups, half, wide), F32),
                 pltpu.VMEM((groups, 1, picks), jnp.int32),
                 pltpu.VMEM((groups, 2, chips, deep, wide), BF16),
@@ -383,8 +429,8 @@
                 collective_id=0, has_side_effects=True, vmem_limit_bytes=40 * 1024 * 1024
             ),
         )(
-            rhs_leaf[0], diag_inv[0, 0], sub_block[0, 0], coupling[0],
-            update_rows, rhs_sep, sep_inv,
+            rhs_leaf[0].T, diag_inv[0, 0], sub_block[0, 0], coupling[0],
+            update_rows, rhs_sep.T, sep_inv,
         )
         return out.T[None], sol.T
 

time: 44 us -> 45.2 us (1.027)
  local copies, waits for them, and re-layouts: 4.06 us -> 7.16 us
  Pallas kernels: 39 us -> 37.1 us
    unnamed x14 -> x16, local copies, waits for them, and re-layouts: 4.06 us -> 7.16 us
    pallas_call x1, Pallas kernels: 39 us -> 37.1 us  [shards(): pl.pallas_call(functools.partial(kernel, groups, chips, skips), out_shape...]
where the time goes in v2:
time: 45.2 us; the launch traced here: 44.9 us
  Pallas kernels  37.1 us (82%)
  local copies, waits for them, and re-layouts  7.16 us (16%)
  between operations  0.66 us (1%)
    pallas_call x1, Pallas kernels, shards(): pl.pallas_call(functools.partial(kernel, groups, chips, skips), out_shape...  37.1 us
    unnamed x16, local copies, waits for them, and re-layouts  7.16 us

profile of v2, /device:TPU:0, one launch (start us, length us, event | category | flops | bytes accessed | tf_op | source)
XLA Modules:
  0.0 44.9 jit_solution(7475986462138229479)
XLA Ops:
  0.6 0.0 copy-start.6
  0.6 0.7 %copy-done.6 = s32[1,256]{1,0:T(1,128)S(1)} copy-done((s32[1,256]{1,0:T(1,128)S(1)}, s32[1,256]{1,0:T(1,128)}, u32[]{:S(2)}) %copy-start.6) | copy-done | bytes 1048
  1.3 0.0 copy-start
  1.3 0.9 %copy-done = bf16[1,1,256,256]{3,2,1,0:T(8,128)(2,1)S(1)} copy-done((bf16[1,1,256,256]{3,2,1,0:T(8,128)(2,1)S(1)}, bf16[1,1,256,256]{3,2,1,0:T(8,128)(2,1)}, u32[]{:S(2)}) %copy-start) | copy-done | bytes 131096
  2.2 0.0 copy-start.1
  2.2 0.9 %copy-done.1 = bf16[1,1,256,256]{3,2,1,0:T(8,128)(2,1)S(1)} copy-done((bf16[1,1,256,256]{3,2,1,0:T(8,128)(2,1)S(1)}, bf16[1,1,256,256]{3,2,1,0:T(8,128)(2,1)}, u32[]{:S(2)}) %copy-start.1) | copy-done | bytes 131096
  3.1 0.0 copy-start.2
  3.1 0.9 %copy-done.2 = bf16[1,256,256]{2,1,0:T(8,128)(2,1)S(1)} copy-done((bf16[1,256,256]{2,1,0:T(8,128)(2,1)S(1)}, bf16[1,256,256]{2,1,0:T(8,128)(2,1)}, u32[]{:S(2)}) %copy-start.2) | copy-done | bytes 131096
  4.0 0.0 copy-start.3
  4.0 0.8 %copy-done.3 = f32[1,256,64]{1,2,0:T(8,128)S(1)} copy-done((f32[1,256,64]{1,2,0:T(8,128)S(1)}, f32[1,256,64]{1,2,0:T(8,128)}, u32[]{:S(2)}) %copy-start.3) | copy-done | bytes 65560
  4.9 0.0 copy-start.4
  4.9 0.8 %copy-done.4 = f32[256,64]{0,1:T(8,128)S(1)} copy-done((f32[256,64]{0,1:T(8,128)S(1)}, f32[256,64]{0,1:T(8,128)}, u32[]{:S(2)}) %copy-start.4) | copy-done | bytes 65560
  5.7 0.0 copy-start.5
  5.7 0.8 %copy-done.5 = bf16[128,256]{1,0:T(8,128)(2,1)S(1)} copy-done((bf16[128,256]{1,0:T(8,128)(2,1)S(1)}, bf16[128,256]{1,0:T(8,128)(2,1)}, u32[]{:S(2)}) %copy-start.5) | copy-done | bytes 65560
  6.5 37.1 %shard_map.86 = (f32[64,256]{1,0:T(8,128)S(1)}, f32[64,256]{1,0:T(8,128)S(1)}) custom-call(f32[64,256]{1,0:T(8,128)S(1)} %bitcast.14, bf16[256,256]{1,0:T(8,128)(2,1)S(1)} %bitcast.11, bf16[256,256]{1,0:T(8,128)(2,1)S(1)} %bitcast.12, bf16[256,256]{1,0:T(8,128)(2,1)S(1)} %bitcast.13, s32[1,256]{1,0:T(1,128)S(1)} %copy-done.6, f32[64,256]{1,0:T(8,128)S(1)} %bitcast.15, ...), custom_call_target="tpu_custom_call" | custom-call | tf_op jit(solution)/shard_map/pallas_call | solution.py:392
  43.6 0.6 %copy.11 = f32[1,256,64]{1,2,0:T(8,128)} copy(f32[1,256,64]{1,2,0:T(8,128)S(1)} %bitcast.17) | data formatting | bytes 131072
  44.3 0.6 %copy.12 = f32[256,64]{0,1:T(8,128)} copy(f32[256,64]{0,1:T(8,128)S(1)} %bitcast.16) | data formatting | bytes 131072
Async XLA Ops:
  0.6 0.7 %copy-start.6 = (s32[1,256]{1,0:T(1,128)S(1)}, s32[1,256]{1,0:T(1,128)}, u32[]{:S(2)}) copy-start(s32[1,256]{1,0:T(1,128)} %idx_ref.1) | copy-start | bytes 3076
  1.3 0.9 %copy-start = (bf16[1,1,256,256]{3,2,1,0:T(8,128)(2,1)S(1)}, bf16[1,1,256,256]{3,2,1,0:T(8,128)(2,1)}, u32[]{:S(2)}) copy-start(bf16[1,1,256,256]{3,2,1,0:T(8,128)(2,1)} %param.8) | copy-start | bytes 393220
  2.2 0.9 %copy-start.1 = (bf16[1,1,256,256]{3,2,1,0:T(8,128)(2,1)S(1)}, bf16[1,1,256,256]{3,2,1,0:T(8,128)(2,1)}, u32[]{:S(2)}) copy-start(bf16[1,1,256,256]{3,2,1,0:T(8,128)(2,1)} %param.9) | copy-start | bytes 393220
  3.1 0.9 %copy-start.2 = (bf16[1,256,256]{2,1,0:T(8,128)(2,1)S(1)}, bf16[1,256,256]{2,1,0:T(8,128)(2,1)}, u32[]{:S(2)}) copy-start(bf16[1,256,256]{2,1,0:T(8,128)(2,1)} %param.10) | copy-start | bytes 393220
  4.0 0.8 %copy-start.3 = (f32[1,256,64]{1,2,0:T(8,128)S(1)}, f32[1,256,64]{1,2,0:T(8,128)}, u32[]{:S(2)}) copy-start(f32[1,256,64]{1,2,0:T(8,128)} %param.7) | copy-start | bytes 196612
  4.9 0.8 %copy-start.4 = (f32[256,64]{0,1:T(8,128)S(1)}, f32[256,64]{0,1:T(8,128)}, u32[]{:S(2)}) copy-start(f32[256,64]{0,1:T(8,128)} %param.12) | copy-start | bytes 196612
  5.7 0.8 %copy-start.5 = (bf16[128,256]{1,0:T(8,128)(2,1)S(1)}, bf16[128,256]{1,0:T(8,128)(2,1)}, u32[]{:S(2)}) copy-start(bf16[128,256]{1,0:T(8,128)(2,1)} %sp_ref.1) | copy-start | bytes 196612

commit v3 on v2

--- a/solution.py
+++ b/solution.py
@@ -46,18 +46,20 @@
 
 
 def through(x, w, multiply):
+    head, rest = w
     both = halves(x)
-    return joined(multiply(both, w[0])) + multiply(both[: x.shape[0]], w[1])
+    return joined(multiply(both, head)) + multiply(both[: x.shape[0]], rest)
 
 
 def kernel(
     groups, chips, skips,
     r_ref, d_ref, b_ref, c_ref, idx_ref, rs_ref, sp_ref,
     out_ref, sol_ref,
-    fac, gmap, hmap, rbuf, ybuf, yin, uin, uout, ubuf, rsbuf, idxbuf, sepbuf, sel, ssep, solt,
+    fac, maps, later, tbuf, turned_out, rbuf, ybuf, yin, uin, uout, ubuf, rsbuf, idxbuf, sepbuf, sel, ssep, solt,
     zbuf, solbuf, vin, vout, xs, obuf,
     loc_s, swap_s, swap_r, y_s, y_r, u_s, u_r, v_s, v_r,
     ux_s, ux_r, rs_s, rs_r, id_s, id_r, sep_s, sep_r, fwd_s, fwd_r,
+    m_s, m_r, mf_s, mf_r, t_s, t_r,
     z_s, z_r, so_s, so_r, x_s, x_r, sx_s, sx_r,
 ):
     plane = lax.axis_index("leaf")
@@ -100,16 +102,12 @@
         for g in range(groups):
             greet((g, last * 2 + core))
 
-        @pl.when(chip > 0)
-        def _():
-            greet((plane, front - 2))
-
-        @pl.when(chip + 1 < last)
-        def _():
-            greet((plane, front + 2))
-
-    near = (chip > 0).astype(jnp.int32) + (chip + 1 < last).astype(jnp.int32)
-    pl.semaphore_wait(barrier, jnp.where(is_last, groups * chips, groups + 1 + near))
+        for c in range(last):
+            @pl.when(chip != c)
+            def _(c=c):
+                greet((plane, c * 2 + core))
+
+    pl.semaphore_wait(barrier, jnp.where(is_last, groups * chips, groups + last))
 
     swaps = []
     locals_ = []
@@ -122,7 +120,9 @@
         locals_.append(copy)
     mine_rows = pl.ds(pl.multiple_of(core * half, half), half)
     other_rows = pl.ds(pl.multiple_of(other * half, half), half)
-    rbuf[core] = r_ref[mine_rows]
+    copy = pltpu.make_async_copy(r_ref.at[mine_rows], rbuf.at[core], loc_s.at[3])
+    copy.start()
+    locals_.append(copy)
     copy = remote(r_ref.at[other_rows], rbuf.at[core], swap_s.at[3], swap_r.at[3], sibling)
     copy.start()
     swaps.append(copy)
@@ -152,8 +152,8 @@
 
     @pl.when(is_last)
     def _():
-        rsbuf[plane] = rs_ref[mine_rows]
-        idxbuf[plane] = idx_ref[...]
+        pltpu.make_async_copy(rs_ref.at[mine_rows], rsbuf.at[plane], loc_s.at[4]).start()
+        pltpu.make_async_copy(idx_ref, idxbuf.at[plane], loc_s.at[5]).start()
 
         def give(g, to):
             remote(rs_ref.at[mine_rows], rsbuf.at[plane], rs_s.at[g], rs_r.at[plane], to).start()
@@ -167,7 +167,6 @@
         copy.wait_recv()
 
     onward = (plane, jnp.minimum(front + 2, last * 2 + core))
-    behind = (plane, jnp.maximum(front - 2, core))
     y_copy = remote(ybuf.at[2], yin, y_s, y_r, onward)
     u_copy = remote(uout, uin, u_s, u_r, onward)
     u_copies = []
@@ -191,12 +190,38 @@
     early = split(dot(fac[1, 0], fac[0, 0]))
     late = split(dot(fac[1, 1], fac[0, 1]))
     whole = split(dot(late[0], early[0]) + (dot(late[1], early[0]) + dot(late[0], early[1])))
-    gmap[0], gmap[1] = whole
     seen = split(
         dot(fac[2, 1], whole[0]) - dot(fac[2, 0], early[0])
         + (dot(fac[2, 1], whole[1]) - dot(fac[2, 0], early[1]))
     )
-    hmap[0], hmap[1] = seen
+    for part in range(2):
+        maps[part, 0] = whole[part]
+        maps[part, 1] = seen[part]
+
+    def map_copy(c, to):
+        return remote(maps.at[core], later.at[c - 1, core], m_s.at[to], m_r.at[c - 1], (plane, to * 2 + core))
+
+    def turned_copy(c, to):
+        return remote(turned_out, tbuf.at[c - 1], t_s.at[to], t_r.at[c - 1], (plane, to * 2 + core))
+
+    def map_onward(c, k):
+        part = later.at[c - 1, k]
+        return remote(part, part, mf_s.at[c - 1], mf_r.at[c - 1], sibling)
+
+    def to_earlier(action):
+        for c in range(1, last):
+            @pl.when(chip == c)
+            def _(c=c):
+                for to in reversed(range(c)):
+                    action(c, to)
+
+    def from_later(action):
+        for c in reversed(range(1, last)):
+            @pl.when(chip < c)
+            def _(c=c):
+                action(c)
+
+    to_earlier(lambda c, to: map_copy(c, to).start())
 
     @pl.when(is_last)
     def _():
@@ -205,6 +230,8 @@
             remote(rs_ref.at[mine_rows], rsbuf.at[g], rs_s.at[g], rs_r.at[g], to).wait_recv()
 
         peers(take)
+        pltpu.make_async_copy(rs_ref.at[mine_rows], rsbuf.at[plane], loc_s.at[4]).wait()
+        pltpu.make_async_copy(idx_ref, idxbuf.at[plane], loc_s.at[5]).wait()
         for g in range(groups):
             rows = lax.broadcasted_iota(jnp.int32, sel.shape[1:], 0)
             sel[g] = (rows == idxbuf[g]).astype(F32).astype(BF16)
@@ -218,7 +245,7 @@
         y_copy.wait_recv()
 
     heard = yin[...]
-    second = own_second + through(heard, gmap, dot_t)
+    second = own_second + through(heard, whole, dot_t)
     ybuf[1] = second
 
     @pl.when(jnp.logical_and(chip > 0, jnp.logical_not(is_last)))
@@ -226,7 +253,7 @@
         ybuf[2] = second
         y_copy.start()
 
-    update = own_update + through(heard, hmap, dot_t)
+    update = own_update + through(heard, seen, dot_t)
 
     @pl.when(chip > 0)
     def _():
@@ -245,10 +272,21 @@
 
     first = own_first - times_t(times_t(heard, fac[0, 0]), fac[1, 0])
     ybuf[0] = first
-    turned = times(times(first, fac[1, 0]), fac[0, 0]) - through(second, gmap, dot)
+    turned = times(times(first, fac[1, 0]), fac[0, 0]) - through(second, whole, dot)
+    turned_out[...] = turned
+    to_earlier(lambda c, to: turned_copy(c, to).start())
+
+    def pass_on(c):
+        map_copy(c, 0).wait_recv()
+        map_onward(c, core).start()
+
+    from_later(pass_on)
 
     z_copies = [
         remote(zbuf, zbuf, z_s.at[c], z_r, (plane, c * 2 + core)) for c in range(last)
+    ]
+    v_copies = [
+        remote(vout, vin, v_s.at[c], v_r, (plane, c * 2 + core)) for c in range(last)
     ]
     so_copies = [
         remote(solbuf.at[core], solbuf.at[core], so_s.at[c], so_r, (plane, c * 2 + core))
@@ -284,8 +322,13 @@
             def _(part=part):
                 solbuf[core] = part
 
-        zbuf[...] = times(solt[...], sel[plane])
-        for copy in reversed(z_copies):
+        found = times(solt[...], sel[plane])
+        zbuf[...] = found
+        for copy in z_copies:
+            copy.start()
+        vout[...] = turned + through(found, seen, dot)
+        vin[...] = jnp.zeros_like(vin)
+        for copy in v_copies:
             copy.start()
         for copy in so_copies:
             copy.start()
@@ -297,22 +340,18 @@
     picked = halves(zbuf[...])
     a_first = ybuf[0] - joined(jnp.dot(picked, fac[2, 0], preferred_element_type=F32))
     a_second = ybuf[1] - joined(jnp.dot(picked, fac[2, 1], preferred_element_type=F32))
-    v_copy = remote(vout, vin, v_s, v_r, behind)
-    turned = turned + through(zbuf[...], hmap, dot)
-
-    @pl.when(is_last)
-    def _():
-        vin[...] = jnp.zeros_like(vin)
-        vout[...] = turned
-
-    @pl.when(jnp.logical_not(is_last))
-    def _():
-        v_copy.wait_recv()
-        vout[...] = turned + through(vin[...], gmap, dot)
-
-    @pl.when(chip > 0)
-    def _():
-        v_copy.start()
+
+    @pl.when(jnp.logical_not(is_last))
+    def _():
+        v_copies[0].wait_recv()
+
+    def step_back(c):
+        turned_copy(c, 0).wait_recv()
+        map_onward(c, other).wait_recv()
+        moved = through(zbuf[...], (later[c - 1, 0, 1], later[c - 1, 1, 1]), dot)
+        vin[...] = tbuf[c - 1] + moved + through(vin[...], (later[c - 1, 0, 0], later[c - 1, 1, 0]), dot)
+
+    from_later(step_back)
 
     x_second = times(a_second - vin[...], fac[1, 1])
     x_first = times(a_first - times(x_second, fac[0, 1]), fac[1, 0])
@@ -349,9 +388,9 @@
         y_copy.wait_send()
         u_copy.wait_send()
 
-    @pl.when(chip > 0)
-    def _():
-        v_copy.wait_send()
+    to_earlier(lambda c, to: map_copy(c, to).wait_send())
+    to_earlier(lambda c, to: turned_copy(c, to).wait_send())
+    from_later(lambda c: map_onward(c, core).wait_send())
 
     @pl.when(is_last)
     def _():
@@ -367,7 +406,7 @@
             remote(part, part, fwd_s.at[g], fwd_r.at[g], sibling).wait_send()
         for copy in z_copies:
             copy.wait_send()
-        for copy in so_copies:
+        for copy in v_copies + so_copies:
             copy.wait_send()
 
     x_copy.wait_send()
@@ -387,7 +426,7 @@
         half = columns // 2
         skips = tuple(g * wide // (2 * deep) for g in range(groups))
         vmem = pl.BlockSpec(memory_space=pltpu.VMEM)
-        anywhere = pl.BlockSpec(memory_space=pl.ANY)
+        hbm = pl.BlockSpec(memory_space=pltpu.HBM)
         dma = pltpu.SemaphoreType.DMA
         out, sol = pl.pallas_call(
             functools.partial(kernel, groups, chips, skips),
@@ -395,12 +434,14 @@
                 jax.ShapeDtypeStruct((columns, width), F32),
                 jax.ShapeDtypeStruct((columns, wide), F32),
             ),
-            in_specs=[vmem, anywhere, anywhere, anywhere, vmem, vmem, anywhere],
+            in_specs=[hbm] * 7,
             out_specs=(vmem, vmem),
             scratch_shapes=[
                 pltpu.VMEM((3, 2, width, width), BF16),
-                pltpu.VMEM((2, width, width), BF16),
-                pltpu.VMEM((2, picks, width), BF16),
+                pltpu.VMEM((2, 2, width, width), BF16),
+                pltpu.VMEM((chips - 2, 2, 2, width, width), BF16),
+                pltpu.VMEM((chips - 2, half, width), F32),
+                pltpu.VMEM((half, width), F32),
                 pltpu.VMEM((2, half, width), F32),
                 pltpu.VMEM((3, half, width), F32),
                 pltpu.VMEM((half, width), F32),
@@ -419,14 +460,15 @@
                 pltpu.VMEM((half, width), F32),
                 pltpu.VMEM((2, half, width), F32),
                 pltpu.VMEM((2, half, width), F32),
-                dma((3,)), dma((4,)), dma((4,)), dma, dma, dma, dma, dma, dma,
+                dma((6,)), dma((4,)), dma((4,)), dma, dma, dma, dma, dma((chips,)), dma,
                 dma((groups,)), dma((groups,)), dma((groups,)), dma((groups,)),
                 dma((groups,)), dma((groups,)), dma((groups,)), dma((groups,)),
                 dma((groups,)), dma((groups,)),
+                dma((chips,)), dma((chips,)), dma((chips,)), dma((chips,)), dma((chips,)), dma((chips,)),
                 dma((chips,)), dma, dma((chips,)), dma, dma, dma, dma, dma,
             ],
             compiler_params=pltpu.CompilerParams(
-                collective_id=0, has_side_effects=True, vmem_limit_bytes=40 * 1024 * 1024
+                collective_id=0, has_side_effects=True, vmem_limit_bytes=64 * 1024 * 1024
             ),
         )(
             rhs_leaf[0].T, diag_inv[0, 0], sub_block[0, 0], coupling[0],

time: 45.2 us -> 39.2 us (0.87)
  local copies, waits for them, and re-layouts: 7.16 us -> 2.14 us
  Pallas kernels: 37.1 us -> 36.2 us
    unnamed x16 -> x4, local copies, waits for them, and re-layouts: 7.16 us -> 2.14 us
    pallas_call x1, Pallas kernels: 37.1 us -> 36.2 us  [shards(): pl.pallas_call(functools.partial(kernel, groups, chips, skips), out_shape...]
where the time goes in v3:
time: 39.2 us; the launch traced here: 39 us
  Pallas kernels  36.2 us (92%)
  local copies, waits for them, and re-layouts  2.14 us (5%)
  between operations  0.65 us (2%)
    pallas_call x1, Pallas kernels, shards(): pl.pallas_call(functools.partial(kernel, groups, chips, skips), out_shape...  36.2 us
    unnamed x4, local copies, waits for them, and re-layouts  2.14 us

profile of v3, /device:TPU:0, one launch (start us, length us, event | category | flops | bytes accessed | tf_op | source)
XLA Modules:
  0.0 39.0 jit_solution(3420777419192181945)
XLA Ops:
  0.6 36.2 %shard_map.86 = (f32[64,256]{1,0:T(8,128)}, f32[64,256]{1,0:T(8,128)}) custom-call(f32[64,256]{1,0:T(8,128)} %bitcast.14, bf16[256,256]{1,0:T(8,128)(2,1)} %bitcast.11, bf16[256,256]{1,0:T(8,128)(2,1)} %bitcast.12, bf16[256,256]{1,0:T(8,128)(2,1)} %bitcast.13, s32[1,256]{1,0:T(1,128)} %idx_ref.1, f32[64,256]{1,0:T(8,128)} %bitcast.15, bf16[128,256]{1,0:T(8,128)(2,1)} %sp_ref.1), custom_call_target="tpu_custom_call" | custom-call | tf_op jit(solution)/shard_map/pallas_call | solution.py:431
  36.9 0.0 copy-start
  36.9 1.5 %copy.11 = f32[1,256,64]{1,2,0:T(8,128)} copy(f32[1,256,64]{1,2,0:T(8,128)} %bitcast.17) | data formatting | bytes 131072
  38.4 0.0 copy-done
  38.4 0.6 %copy.12 = f32[256,64]{0,1:T(8,128)} copy(f32[256,64]{0,1:T(8,128)S(1)} %bitcast.16) | data formatting | bytes 131072
Async XLA Ops:
  36.9 1.5 %copy-start = (f32[64,256]{1,0:T(8,128)S(1)}, f32[64,256]{1,0:T(8,128)}, u32[]{:S(2)}) copy-start(f32[64,256]{1,0:T(8,128)} %get-tuple-element.5) | copy-start | bytes 196612

commit v4 on v3

--- a/solution.py
+++ b/solution.py
@@ -221,8 +221,6 @@
             def _(c=c):
                 action(c)
 
-    to_earlier(lambda c, to: map_copy(c, to).start())
-
     @pl.when(is_last)
     def _():
         def take(g, to):
@@ -274,6 +272,7 @@
     ybuf[0] = first
     turned = times(times(first, fac[1, 0]), fac[0, 0]) - through(second, whole, dot)
     turned_out[...] = turned
+    to_earlier(lambda c, to: map_copy(c, to).start())
     to_earlier(lambda c, to: turned_copy(c, to).start())
 
     def pass_on(c):

time: 39.2 us -> 35.4 us (0.903)
  Pallas kernels: 36.2 us -> 32.5 us
    pallas_call x1, Pallas kernels: 36.2 us -> 32.5 us  [shards(): pl.pallas_call(functools.partial(kernel, groups, chips, skips), out_shape...]
where the time goes in v4:
time: 35.4 us; the launch traced here: 35.2 us
  Pallas kernels  32.5 us (92%)
  local copies, waits for them, and re-layouts  2.14 us (6%)
  between operations  0.65 us (2%)
    pallas_call x1, Pallas kernels, shards(): pl.pallas_call(functools.partial(kernel, groups, chips, skips), out_shape...  32.5 us
    unnamed x4, local copies, waits for them, and re-layouts  2.14 us

profile of v4, /device:TPU:0, one launch (start us, length us, event | category | flops | bytes accessed | tf_op | source)
XLA Modules:
  0.0 35.2 jit_solution(3724354968920502236)
XLA Ops:
  0.6 32.5 %shard_map.86 = (f32[64,256]{1,0:T(8,128)}, f32[64,256]{1,0:T(8,128)}) custom-call(f32[64,256]{1,0:T(8,128)} %bitcast.14, bf16[256,256]{1,0:T(8,128)(2,1)} %bitcast.11, bf16[256,256]{1,0:T(8,128)(2,1)} %bitcast.12, bf16[256,256]{1,0:T(8,128)(2,1)} %bitcast.13, s32[1,256]{1,0:T(1,128)} %idx_ref.1, f32[64,256]{1,0:T(8,128)} %bitcast.15, bf16[128,256]{1,0:T(8,128)(2,1)} %sp_ref.1), custom_call_target="tpu_custom_call" | custom-call | tf_op jit(solution)/shard_map/pallas_call | solution.py:430
  33.1 0.0 copy-start
  33.1 1.5 %copy.11 = f32[1,256,64]{1,2,0:T(8,128)} copy(f32[1,256,64]{1,2,0:T(8,128)} %bitcast.17) | data formatting | bytes 131072
  34.6 0.0 copy-done
  34.6 0.6 %copy.12 = f32[256,64]{0,1:T(8,128)} copy(f32[256,64]{0,1:T(8,128)S(1)} %bitcast.16) | data formatting | bytes 131072
Async XLA Ops:
  33.1 1.5 %copy-start = (f32[64,256]{1,0:T(8,128)S(1)}, f32[64,256]{1,0:T(8,128)}, u32[]{:S(2)}) copy-start(f32[64,256]{1,0:T(8,128)} %get-tuple-element.5) | copy-start | bytes 196612

commit v5 on v4

--- a/solution.py
+++ b/solution.py
@@ -107,22 +107,22 @@
             def _(c=c):
                 greet((plane, c * 2 + core))
 
+    mine_rows = pl.ds(pl.multiple_of(core * half, half), half)
+    other_rows = pl.ds(pl.multiple_of(other * half, half), half)
+    locals_ = [
+        pltpu.make_async_copy(ref, fac.at[i, core], loc_s.at[i])
+        for i, ref in enumerate((b_ref, d_ref, c_ref))
+    ]
+    locals_.append(pltpu.make_async_copy(r_ref.at[mine_rows], rbuf.at[core], loc_s.at[3]))
+    for copy in locals_:
+        copy.start()
     pl.semaphore_wait(barrier, jnp.where(is_last, groups * chips, groups + last))
 
     swaps = []
-    locals_ = []
     for i, ref in enumerate((b_ref, d_ref, c_ref)):
         copy = remote(ref, fac.at[i, core], swap_s.at[i], swap_r.at[i], sibling)
         copy.start()
         swaps.append(copy)
-        copy = pltpu.make_async_copy(ref, fac.at[i, core], loc_s.at[i])
-        copy.start()
-        locals_.append(copy)
-    mine_rows = pl.ds(pl.multiple_of(core * half, half), half)
-    other_rows = pl.ds(pl.multiple_of(other * half, half), half)
-    copy = pltpu.make_async_copy(r_ref.at[mine_rows], rbuf.at[core], loc_s.at[3])
-    copy.start()
-    locals_.append(copy)
     copy = remote(r_ref.at[other_rows], rbuf.at[core], swap_s.at[3], swap_r.at[3], sibling)
     copy.start()
     swaps.append(copy)
@@ -233,40 +233,40 @@
         for g in range(groups):
             rows = lax.broadcasted_iota(jnp.int32, sel.shape[1:], 0)
             sel[g] = (rows == idxbuf[g]).astype(F32).astype(BF16)
+
+    @pl.when(chip > 0)
+    def _():
+        y_copy.wait_recv()
+
+    heard = yin[...]
+    second = own_second + through(heard, whole, dot_t)
+    ybuf[1] = second
+
+    @pl.when(jnp.logical_and(chip > 0, jnp.logical_not(is_last)))
+    def _():
+        ybuf[2] = second
+        y_copy.start()
+
+    update = own_update + through(heard, seen, dot_t)
+
+    @pl.when(chip > 0)
+    def _():
+        u_copy.wait_recv()
+
+    uout[...] = update + uin[...]
+
+    @pl.when(jnp.logical_not(is_last))
+    def _():
+        u_copy.start()
+
+    @pl.when(is_last)
+    def _():
+        for step in range(1, groups):
+            u_copies[step - 1].start()
         for g in range(groups):
             part = sepbuf.at[g, core, pl.ds(skips[g], chips - skips[g])]
             pltpu.make_async_copy(part, part, sep_r.at[g]).wait()
             remote(part, part, fwd_s.at[g], fwd_r.at[g], sibling).start()
-
-    @pl.when(chip > 0)
-    def _():
-        y_copy.wait_recv()
-
-    heard = yin[...]
-    second = own_second + through(heard, whole, dot_t)
-    ybuf[1] = second
-
-    @pl.when(jnp.logical_and(chip > 0, jnp.logical_not(is_last)))
-    def _():
-        ybuf[2] = second
-        y_copy.start()
-
-    update = own_update + through(heard, seen, dot_t)
-
-    @pl.when(chip > 0)
-    def _():
-        u_copy.wait_recv()
-
-    uout[...] = update + uin[...]
-
-    @pl.when(jnp.logical_not(is_last))
-    def _():
-        u_copy.start()
-
-    @pl.when(is_last)
-    def _():
-        for step in range(1, groups):
-            u_copies[step - 1].start()
 
     first = own_first - times_t(times_t(heard, fac[0, 0]), fac[1, 0])
     ybuf[0] = first

time: 35.4 us -> 35.8 us (1.011)
    pallas_call x1, Pallas kernels: 32.5 us -> 32.8 us  [shards(): pl.pallas_call(functools.partial(kernel, groups, chips, skips), out_shape...]
where the time goes in v5:
time: 35.8 us; the launch traced here: 35.6 us
  Pallas kernels  32.8 us (92%)
  local copies, waits for them, and re-layouts  2.14 us (6%)
  between operations  0.65 us (2%)
    pallas_call x1, Pallas kernels, shards(): pl.pallas_call(functools.partial(kernel, groups, chips, skips), out_shape...  32.8 us
    unnamed x4, local copies, waits for them, and re-layouts  2.14 us

profile of v5, /device:TPU:0, one launch (start us, length us, event | category | flops | bytes accessed | tf_op | source)
XLA Modules:
  0.0 35.6 jit_solution(8764448557236221468)
XLA Ops:
  0.6 32.8 %shard_map.86 = (f32[64,256]{1,0:T(8,128)}, f32[64,256]{1,0:T(8,128)}) custom-call(f32[64,256]{1,0:T(8,128)} %bitcast.14, bf16[256,256]{1,0:T(8,128)(2,1)} %bitcast.11, bf16[256,256]{1,0:T(8,128)(2,1)} %bitcast.12, bf16[256,256]{1,0:T(8,128)(2,1)} %bitcast.13, s32[1,256]{1,0:T(1,128)} %idx_ref.1, f32[64,256]{1,0:T(8,128)} %bitcast.15, bf16[128,256]{1,0:T(8,128)(2,1)} %sp_ref.1), custom_call_target="tpu_custom_call" | custom-call | tf_op jit(solution)/shard_map/pallas_call | solution.py:430
  33.5 0.0 copy-start
  33.5 1.5 %copy.11 = f32[1,256,64]{1,2,0:T(8,128)} copy(f32[1,256,64]{1,2,0:T(8,128)} %bitcast.17) | data formatting | bytes 131072
  35.0 0.0 copy-done
  35.0 0.6 %copy.12 = f32[256,64]{0,1:T(8,128)} copy(f32[256,64]{0,1:T(8,128)S(1)} %bitcast.16) | data formatting | bytes 131072
Async XLA Ops:
  33.5 1.5 %copy-start = (f32[64,256]{1,0:T(8,128)S(1)}, f32[64,256]{1,0:T(8,128)}, u32[]{:S(2)}) copy-start(f32[64,256]{1,0:T(8,128)} %get-tuple-element.5) | copy-start | bytes 196612
